TPU v7x, 32 devices: a whole 2x2x4 slice. The times are simulated.
32 devices in a mesh: member: 8 (over z, x), dp: 4 (over y, core).
Axes of the slice: x: 2, y: 2, z: 4, core: 2. Of those that a mesh axis runs over, the one named last changes fastest.
Arguments:
- feature_pool: bfloat16 [2048, 256], P('dp'), may hold values from -6 to 6
- labels: int32 [2048], P('dp'), may hold values from 0 to 9
- sample_rows: int32 [1024], P('dp'), may hold values from 0 to 511
- noise_variance: float32 [10], replicated, may hold values from 160 to 640
- first_weight: bfloat16 [16, 256, 2048], P('member', None, 'dp'), may hold values from -6 to 6
- middle_weight: bfloat16 [16, 2048, 2048], P('member', 'dp'), may hold values from -6 to 6
- last_weight: bfloat16 [16, 2048, 10], P('member', 'dp'), may hold values from -6 to 6
Outputs:
- new_first: bfloat16 [16, 256, 2048], P('member', None, 'dp')
- new_middle: bfloat16 [16, 2048, 2048], P('member', 'dp')
- new_last: bfloat16 [16, 2048, 10], P('member', 'dp')
Inputs may be any that keep to these rules, and one draw needn't show every extreme that they name: Sample i reads pool row (i // 256) * 512 + sample_rows[i]. `labels`: class index of each pool row.
All inputs are finite; a program needn't handle non-finite values.
Results may differ from a plain program's by a relative error of at most 0.013.
Values may be sent and summed in bfloat16 or wider, within the bound.
No kernel may reach another device: no remote copies, remote signals or barrier semaphores. Data moves between devices by JAX's collectives and lax.ppermute only.
A program may use at most 128 MiB of HBM per device.

v0:
```python
import jax
import jax.numpy as jnp
from jax import lax
from jax.sharding import PartitionSpec as P

F_IN = 256
H = 2048
precise = lax.Precision.HIGHEST


def update_piece(piece, mixing):
    ensemble = piece.shape[0]
    flat = piece.reshape(ensemble, -1)
    upper = mixing.astype(jnp.bfloat16)
    lower = (mixing - upper.astype(jnp.float32)).astype(jnp.bfloat16)
    stacked = jnp.concatenate([upper.T, lower.T], axis=0)
    both = jnp.dot(stacked, flat, preferred_element_type=jnp.float32)
    product = both[:ensemble] + both[ensemble:]
    column_total = jnp.sum(mixing, axis=0)
    average = jnp.sum(flat, axis=0, dtype=jnp.float32) / ensemble
    renewed = flat.astype(jnp.float32) + product - column_total[:, None] * average[None, :]
    return renewed.astype(jnp.bfloat16).reshape(piece.shape)


def on_device(
    feature_pool, labels, sample_rows, noise_variance, first_weight, middle_weight, last_weight
):
    local_count = sample_rows.shape[0]
    members_here = first_weight.shape[0]
    classes_total = noise_variance.shape[0]
    in_scale = F_IN ** (-0.5)
    hid_scale = H ** (-0.5)
    inputs = feature_pool[sample_rows]
    classes = labels[sample_rows]
    target = (classes[:, None] == jnp.arange(classes_total, dtype=jnp.int32)[None, :]).astype(
        jnp.float32
    )
    first_full, middle_full, last_full = (
        lax.all_gather(first_weight, "dp", axis=2, tiled=True),
        lax.all_gather(middle_weight, "dp", axis=1, tiled=True),
        lax.all_gather(last_weight, "dp", axis=1, tiled=True),
    )
    hidden_one = jnp.tanh(
        jnp.einsum("sf,jfh->jsh", inputs, first_full, preferred_element_type=jnp.float32) * in_scale
    ).astype(jnp.bfloat16)
    hidden_two = jnp.tanh(
        jnp.einsum("jsk,jkh->jsh", hidden_one, middle_full, preferred_element_type=jnp.float32)
        * hid_scale
    ).astype(jnp.bfloat16)
    outputs = (
        jnp.einsum("jsh,jhc->jsc", hidden_two, last_full, preferred_element_type=jnp.float32)
        * hid_scale
    )
    whiten = 1.0 / jnp.sqrt(noise_variance)
    scaled = (outputs * whiten).reshape(members_here, local_count * classes_total)
    observed = (target * whiten).reshape(local_count * classes_total)
    every_member = lax.all_gather(scaled, "member", axis=0, tiled=True)
    center = jnp.mean(every_member, axis=0)
    anomaly = every_member - center
    gram_part = jnp.dot(anomaly, anomaly.T, precision=precise)
    drive_part = jnp.dot(anomaly, observed - center, precision=precise)
    gram_matrix, drive = (
        lax.psum(gram_part.astype(jnp.bfloat16), "dp").astype(jnp.float32),
        lax.psum(drive_part.astype(jnp.bfloat16), "dp").astype(jnp.float32),
    )
    ensemble = gram_matrix.shape[0]
    system = gram_matrix + ensemble * jnp.eye(ensemble, dtype=jnp.float32)
    factor = jnp.linalg.cholesky(system)
    mixing = jax.scipy.linalg.cho_solve((factor, True), drive[:, None] - gram_matrix)
    grouped = (
        lax.all_to_all(first_weight, "member", split_axis=1, concat_axis=0, tiled=True),
        lax.all_to_all(middle_weight, "member", split_axis=1, concat_axis=0, tiled=True),
        lax.all_to_all(last_weight, "member", split_axis=1, concat_axis=0, tiled=True),
    )
    updated = (
        update_piece(grouped[0], mixing),
        update_piece(grouped[1], mixing),
        update_piece(grouped[2], mixing),
    )
    new_first, new_middle, new_last = (
        lax.all_to_all(updated[0], "member", split_axis=0, concat_axis=1, tiled=True),
        lax.all_to_all(updated[1], "member", split_axis=0, concat_axis=1, tiled=True),
        lax.all_to_all(updated[2], "member", split_axis=0, concat_axis=1, tiled=True),
    )
    return (new_first, new_middle, new_last)


def solution(mesh):
    in_specs = (
        P("dp", None),
        P("dp"),
        P("dp"),
        P(),
        P("member", None, "dp"),
        P("member", "dp", None),
        P("member", "dp", None),
    )
    out_specs = (P("member", None, "dp"), P("member", "dp", None), P("member", "dp", None))
    return jax.shard_map(
        on_device, mesh=mesh, in_specs=in_specs, out_specs=out_specs, check_vma=False
    )
```

profile of v0, /device:TPU:0, one launch (start us, length us, event | category | flops | bytes accessed | tf_op | source)
XLA Modules:
  0.0 349.3 jit_solution(2352689093779938661)
XLA Ops:
  7.2 0.7 all-gather.4.cloned.1.call-update
  8.0 0.7 all-gather.6.cloned.1.call-update
  8.7 0.2 copy.49
  8.9 1.0 reshape.116
  9.9 7.3 %all-to-all-start.4 = ((bf16[8,2,640]{2,1,0:T(2,128)(2,1)}), bf16[8,2,640]{2,1,0:T(2,128)(2,1)S(1)}, u32[]{:S(2)}, u32[]{:S(2)}) async-start(bf16[8,2,640]{2,1,0:T(2,128)(2,1)} %reshape.116), calls=%async_computation.4 | async-start | bytes 40960 | tf_op jit(solution)/shard_map/all_to_all | solution.py:73
  17.2 1.3 copy.40
  18.5 5.3 %all-to-all-done.4 = bf16[8,2,640]{2,1,0:T(2,128)(2,1)S(1)} async-done(((bf16[8,2,640]{2,1,0:T(2,128)(2,1)}), bf16[8,2,640]{2,1,0:T(2,128)(2,1)S(1)}, u32[]{:S(2)}, u32[]{:S(2)}) %all-to-all-start.4) | async-done | bytes 20512 | tf_op jit(solution)/shard_map/all_to_all | solution.py:73
  23.8 3.5 %all-to-all-start = ((bf16[2,256,512]{2,0,1:T(2,128)(2,1)}), bf16[2,256,512]{2,0,1:T(2,128)(2,1)S(1)}, u32[]{:S(2)}, u32[]{:S(2)}) async-start(bf16[2,256,512]{2,0,1:T(2,128)(2,1)} %copy.40), calls=%async_computation | async-start | bytes 1048576 | tf_op jit(solution)/shard_map/all_to_all | solution.py:71
  27.3 8.5 %copy.46 = bf16[2,512,2048]{2,0,1:T(2,128)(2,1)} copy(bf16[2,512,2048]{2,1,0:T(8,128)(2,1)} %param.12) | data formatting | bytes 8388608 | tf_op args[5]
  35.8 4.7 %all-to-all-done = bf16[2,256,512]{2,0,1:T(2,128)(2,1)S(1)} async-done(((bf16[2,256,512]{2,0,1:T(2,128)(2,1)}), bf16[2,256,512]{2,0,1:T(2,128)(2,1)S(1)}, u32[]{:S(2)}, u32[]{:S(2)}) %all-to-all-start) | async-done | bytes 524320 | tf_op jit(solution)/shard_map/all_to_all | solution.py:71
  40.5 4.6 %all-to-all-start.2 = ((bf16[2,512,2048]{2,0,1:T(2,128)(2,1)}), bf16[2,512,2048]{2,0,1:T(2,128)(2,1)}, u32[]{:S(2)}, u32[]{:S(2)}) async-start(bf16[2,512,2048]{2,0,1:T(2,128)(2,1)} %copy.46), calls=%async_computation.2 | async-start | bytes 8388608 | tf_op jit(solution)/shard_map/all_to_all | solution.py:72
  45.3 1.8 gather_fusion
  47.1 1.9 gather_fusion.1
  49.0 0.5 fusion.32
  49.5 0.1 fusion.12
  49.6 0.1 mul.94
  49.8 6.5 %all_gather.14 = bf16[2,2048,10]{1,2,0:T(8,128)(2,1)S(1)} all-gather(bf16[2,512,10]{1,2,0:T(8,128)(2,1)S(1)} %copy.42), channel_id=1, replica_groups=mesh['member'=8,'dp'=4] {'dp'}, dimensions={1}, use_global_device_ids=true | all-gather | bytes 102400 | tf_op jit(solution)/shard_map/all_gather | solution.py:41
  56.2 0.5 reshape.117
  56.8 0.9 reshape.90
  57.8 0.1 div.51
  58.0 0.3 copy.53
  58.4 0.6 copy.54
  59.1 77.7 %all-to-all-done.2 = bf16[2,512,2048]{2,0,1:T(2,128)(2,1)} async-done(((bf16[2,512,2048]{2,0,1:T(2,128)(2,1)}), bf16[2,512,2048]{2,0,1:T(2,128)(2,1)}, u32[]{:S(2)}, u32[]{:S(2)}) %all-to-all-start.2) | async-done | bytes 4194336 | tf_op jit(solution)/shard_map/all_to_all | solution.py:72
  136.8 4.1 %copy.47 = bf16[2,8,64,2048]{3,2,0,1:T(8,128)(2,1)S(1)} copy(bf16[2,8,64,2048]{3,0,2,1:T(2,128)(2,1)} %bitcast.12) | data formatting | bytes 8388608 | tf_op jit(solution)/shard_map/all_to_all | solution.py:72
  140.9 4.3 %copy.56 = bf16[2,8,64,2048]{3,1,2,0:T(8,128)(2,1)} copy(bf16[2,8,64,2048]{3,2,1,0:T(8,128)(2,1)S(1)} %bitcast.93) | data formatting | bytes 8388608
  145.2 4.2 %convert_reduce_fusion = f32[64,2048]{1,0:T(8,128)S(1)} fusion(bf16[2,8,64,2048]{3,0,2,1:T(2,128)(2,1)} %bitcast.12), kind=kLoop, calls=%fused_computation.6 | loop fusion | flops 4063232 | bytes 4718592 | tf_op jit(solution)/shard_map/reduce_sum | solution.py:20
  149.5 0.1 copy.57
  149.6 9.9 %tanh_convert_fusion = bf16[2,256,2048]{2,1,0:T(8,128)(2,1)S(1)} fusion(bf16[2,2048,2048]{2,1,0:T(8,128)(2,1)} %all-gather.6.cloned.1.call-done, bf16[2,256,2048]{2,1,0:T(8,128)(2,1)} %all-gather.4.cloned.1.call-done, bf16[256,256]{1,0:T(8,128)(2,1)S(1)} %copy-done.5), kind=kOutput, calls=%fused_computation.7 | convolution fusion | flops 4836032512 | bytes 21102592 | tf_op jit(solution)/shard_map/jsk,jkh->jsh/dot_general | solution.py:47
  159.6 1.3 convolution_multiply_fusion
  160.8 0.9 copy.43
  161.7 0.2 reshape.110
  161.9 30.8 %all-gather = f32[8,2,2560]{2,1,0:T(2,128)S(1)} all-gather(f32[1,2,2560]{2,1,0:T(2,128)S(1)} %reshape.110), channel_id=1, replica_groups=mesh['member'=8,'dp'=4] {'member'}, dimensions={0}, use_global_device_ids=true | all-gather | bytes 184320 | tf_op jit(solution)/shard_map/all_gather | solution.py:57
  192.7 0.1 reshape.111
  192.9 0.3 convolution_convert_fusion
  193.2 0.3 fusion.4
  193.5 5.8 %all-reduce = (bf16[16,16]{1,0:T(8,128)(2,1)S(1)}, bf16[16]{0:T(256)(128)(2,1)S(1)}) all-reduce(bf16[16,16]{1,0:T(8,128)(2,1)S(1)} %convolution_convert_fusion, bf16[16]{0:T(256)(128)(2,1)S(1)} %fusion.4), channel_id=1, replica_groups=mesh['member'=8,'dp'=4] {'dp'}, use_global_device_ids=true, to_apply=%region_1.0 | all-reduce | flops 272 | bytes 1088 | tf_op jit(solution)/shard_map/psum | solution.py:63
  199.3 0.1 copy.44
  199.4 1.5 cholesky.16
  200.9 0.6 compare_reduce_fusion
  201.6 0.6 fusion.18
  202.2 1.2 custom-call.10
  203.4 0.2 fusion.19
  203.7 0.2 fusion.20
  203.8 1.0 fusion.28
  204.8 0.8 fusion.17
  205.6 0.5 reshape.91
  206.2 0.2 copy.51
  206.4 0.7 reshape.118
  207.1 3.7 %all-to-all-start.5 = ((bf16[8,2,640]{2,1,0:T(2,128)(2,1)}), bf16[8,2,640]{2,1,0:T(2,128)(2,1)S(1)}, u32[]{:S(2)}, u32[]{:S(2)}) async-start(bf16[8,2,640]{2,1,0:T(2,128)(2,1)} %reshape.118), calls=%async_computation.5 | async-start | bytes 40960 | tf_op jit(solution)/shard_map/all_to_all | solution.py:83
  210.8 0.5 fusion.30
  211.3 1.4 fusion.7
  212.7 0.3 copy-done.3
  213.0 7.0 %fusion.29 = f32[32,131072]{1,0:T(8,128)} fusion(bf16[16,131072]{1,0:T(8,128)(2,1)S(1)} %bitcast.91, bf16[16,16]{0,1:T(8,128)(2,1)S(1)} %get-tuple-element.11, bf16[16,16]{0,1:T(8,128)(2,1)S(1)} %get-tuple-element.8), kind=kOutput, calls=%fused_computation.61 | convolution fusion | flops 134219776 | bytes 20972544 | tf_op jit(solution)/shard_map/dot_general | solution.py:17
  220.0 0.9 copy.55
  221.0 6.0 %all-to-all-start.1 = ((bf16[16,32,512]{2,1,0:T(8,128)(2,1)}), bf16[16,32,512]{2,1,0:T(8,128)(2,1)S(1)}, u32[]{:S(2)}, u32[]{:S(2)}) async-start(bf16[16,32,512]{2,1,0:T(8,128)(2,1)} %bitcast.30), calls=%async_computation.1 | async-start | bytes 1048576 | tf_op jit(solution)/shard_map/all_to_all | solution.py:81
  227.0 7.8 %fusion.2 = bf16[16,131072]{1,0:T(8,128)(2,1)S(1)} fusion(f32[32,131072]{1,0:T(8,128)} %fusion.29, bf16[16,131072]{1,0:T(8,128)(2,1)} %bitcast.90, f32[131072]{0:T(1024)S(1)} %bitcast.102, f32[16]{0:T(128)S(1)} %get-tuple-element.7), kind=kLoop, calls=%fused_computation.5 | loop fusion | flops 12582912 | bytes 25690176 | tf_op jit(solution)/shard_map/convert_element_type | solution.py:22
  234.8 4.3 %copy.58 = bf16[2,8,64,2048]{3,2,1,0:T(8,128)(2,1)} copy(bf16[2,8,64,2048]{3,1,2,0:T(8,128)(2,1)S(1)} %bitcast.94) | data formatting | bytes 8388608
  239.1 1.8 all-to-all-done.1
  240.9 4.6 %all-to-all-start.3 = ((bf16[16,64,2048]{2,1,0:T(8,128)(2,1)}), bf16[16,64,2048]{2,1,0:T(8,128)(2,1)}, u32[]{:S(2)}, u32[]{:S(2)}) async-start(bf16[16,64,2048]{2,1,0:T(8,128)(2,1)} %bitcast.92), calls=%async_computation.3 | async-start | bytes 8388608 | tf_op jit(solution)/shard_map/all_to_all | solution.py:82
  245.5 0.1 reshape.119
  245.6 0.7 all_to_all.92
  246.3 0.8 copy.45
  247.2 90.4 %all-to-all-done.3 = bf16[16,64,2048]{2,1,0:T(8,128)(2,1)} async-done(((bf16[16,64,2048]{2,1,0:T(8,128)(2,1)}), bf16[16,64,2048]{2,1,0:T(8,128)(2,1)}, u32[]{:S(2)}, u32[]{:S(2)}) %all-to-all-start.3) | async-done | bytes 4194336 | tf_op jit(solution)/shard_map/all_to_all | solution.py:82
  337.6 4.8 %copy.48 = bf16[8,2,64,2048]{3,2,0,1:T(8,128)(2,1)} copy(bf16[8,2,64,2048]{3,2,1,0:T(8,128)(2,1)} %bitcast.14) | data formatting | bytes 8388608 | tf_op jit(solution)/shard_map/all_to_all | solution.py:82
  (43 shorter events, 0.6 us)
Async XLA Ops:
  7.2 38.1 %copy-start = (bf16[512,256]{1,0:T(8,128)(2,1)S(1)}, bf16[512,256]{1,0:T(8,128)(2,1)}, u32[]{:S(2)}) copy-start(bf16[512,256]{1,0:T(8,128)(2,1)} %param.7) | copy-start | bytes 786436
  7.2 10.0 %copy-start.4 = (bf16[2,256,512]{2,1,0:T(8,128)(2,1)S(1)}, bf16[2,256,512]{2,1,0:T(8,128)(2,1)}, u32[]{:S(2)}) copy-start(bf16[2,256,512]{2,1,0:T(8,128)(2,1)} %param.11) | copy-start | bytes 1572868
  7.2 1.5 copy-start.6
  7.2 142.4 %all-gather.4.cloned.1.call-start = ((), (), s32[]{:S(2)}) async-start(), calls=%async_computation.6 | async-start | bytes 2621440 | tf_op jit(solution)/shard_map/all_gather | solution.py:39
  7.9 141.7 %all-gather.6.cloned.1.call-start = ((), (), s32[]{:S(2)}) async-start(), calls=%async_computation.7 | async-start | bytes 20971520 | tf_op jit(solution)/shard_map/all_gather | solution.py:40
  9.9 13.9 %all-to-all-start.4 = ((bf16[8,2,640]{2,1,0:T(2,128)(2,1)}), bf16[8,2,640]{2,1,0:T(2,128)(2,1)S(1)}, u32[]{:S(2)}, u32[]{:S(2)}) async-start(bf16[8,2,640]{2,1,0:T(2,128)(2,1)} %reshape.116), calls=%async_computation.4 | async-start | bytes 40960 | tf_op jit(solution)/shard_map/all_to_all | solution.py:73
  23.8 16.8 %all-to-all-start = ((bf16[2,256,512]{2,0,1:T(2,128)(2,1)}), bf16[2,256,512]{2,0,1:T(2,128)(2,1)S(1)}, u32[]{:S(2)}, u32[]{:S(2)}) async-start(bf16[2,256,512]{2,0,1:T(2,128)(2,1)} %copy.40), calls=%async_computation | async-start | bytes 1048576 | tf_op jit(solution)/shard_map/all_to_all | solution.py:71
  35.8 9.4 %copy-start.7 = (s32[256]{0:T(256)S(1)}, s32[256]{0:T(256)}, u32[]{:S(2)}) copy-start(s32[256]{0:T(256)} %param.9) | copy-start | bytes 3076
  35.8 11.2 %copy-start.2 = (s32[512]{0:T(512)S(1)}, s32[512]{0:T(512)}, u32[]{:S(2)}) copy-start(s32[512]{0:T(512)} %param.8) | copy-start | bytes 6148
  35.8 13.2 %copy-start.9 = (f32[10]{0:T(128)S(1)}, f32[10]{0:T(128)}, u32[]{:S(2)}) copy-start(f32[10]{0:T(128)} %param.10) | copy-start | bytes 124
  40.5 96.3 %all-to-all-start.2 = ((bf16[2,512,2048]{2,0,1:T(2,128)(2,1)}), bf16[2,512,2048]{2,0,1:T(2,128)(2,1)}, u32[]{:S(2)}, u32[]{:S(2)}) async-start(bf16[2,512,2048]{2,0,1:T(2,128)(2,1)} %copy.46), calls=%async_computation.2 | async-start | bytes 8388608 | tf_op jit(solution)/shard_map/all_to_all | solution.py:72
  145.2 4.4 %copy-start.5 = (bf16[256,256]{1,0:T(8,128)(2,1)S(1)}, bf16[256,256]{1,0:T(8,128)(2,1)}, u32[]{:S(2)}) copy-start(bf16[256,256]{1,0:T(8,128)(2,1)} %gather_fusion) | copy-start | bytes 393220
  149.6 10.0 %copy-start.8 = (f32[10]{0:T(128)S(1)}, f32[10]{0:T(128)}, u32[]{:S(2)}) copy-start(f32[10]{0:T(128)} %get-tuple-element.10) | copy-start | bytes 124
  207.1 13.9 %all-to-all-start.5 = ((bf16[8,2,640]{2,1,0:T(2,128)(2,1)}), bf16[8,2,640]{2,1,0:T(2,128)(2,1)S(1)}, u32[]{:S(2)}, u32[]{:S(2)}) async-start(bf16[8,2,640]{2,1,0:T(2,128)(2,1)} %reshape.118), calls=%async_computation.5 | async-start | bytes 40960 | tf_op jit(solution)/shard_map/all_to_all | solution.py:83
  210.8 2.2 copy-start.3
  221.0 20.0 %all-to-all-start.1 = ((bf16[16,32,512]{2,1,0:T(8,128)(2,1)}), bf16[16,32,512]{2,1,0:T(8,128)(2,1)S(1)}, u32[]{:S(2)}, u32[]{:S(2)}) async-start(bf16[16,32,512]{2,1,0:T(8,128)(2,1)} %bitcast.30), calls=%async_computation.1 | async-start | bytes 1048576 | tf_op jit(solution)/shard_map/all_to_all | solution.py:81
  240.9 96.7 %all-to-all-start.3 = ((bf16[16,64,2048]{2,1,0:T(8,128)(2,1)}), bf16[16,64,2048]{2,1,0:T(8,128)(2,1)}, u32[]{:S(2)}, u32[]{:S(2)}) async-start(bf16[16,64,2048]{2,1,0:T(8,128)(2,1)} %bitcast.92), calls=%async_computation.3 | async-start | bytes 8388608 | tf_op jit(solution)/shard_map/all_to_all | solution.py:82
  337.6 4.8 %copy-start.1 = (bf16[512,256]{1,0:T(8,128)(2,1)S(1)}, bf16[512,256]{1,0:T(8,128)(2,1)}, u32[]{:S(2)}) copy-start(bf16[512,256]{1,0:T(8,128)(2,1)} %param.7) | copy-start | bytes 786436
Sparse Core Ops, SparseCore 0:
  9.6 25.2 all-gather.3
  36.5 106.5 all-gather.5
where the time goes:
time: 350 us; the launch traced here: 349 us
  waiting for transfers between devices  181 us (52%)
  blocking collectives  43.1 us (12%)
  local copies, waits for them, and re-layouts  40.9 us (12%)
  starting transfers between devices  29.8 us (9%)
  matrix products  20.6 us (6%)
  other arithmetic  19.1 us (5%)
  between operations  14.4 us (4%)
    all_to_all x1, waiting for transfers between devices, on_device(): lax.all_to_all(updated[1], 'member', split_axis=0, concat_axis=1, tiled=T...  90.4 us
    all_to_all x1, waiting for transfers between devices, on_device(): lax.all_to_all(middle_weight, 'member', split_axis=1, concat_axis=0, tile...  77.7 us
    all_gather x1, blocking collectives, on_device(): every_member = lax.all_gather(scaled, 'member', axis=0, tiled=True)  30.8 us
    unnamed x36, local copies, waits for them, and re-layouts  23.7 us
    convert_element_type x3, other arithmetic, update_piece(): return renewed.astype(jnp.bfloat16).reshape(piece.shape)  10 us
    dot_general x1, matrix products, on_device(): jnp.einsum('jsk,jkh->jsh', hidden_one, middle_full, preferred_element_typ...  9.89 us
    dot_general x3, matrix products, update_piece(): both = jnp.dot(stacked, flat, preferred_element_type=jnp.float32)  8.53 us
    all_to_all x1, starting transfers between devices, on_device(): lax.all_to_all(last_weight, 'member', split_axis=1, concat_axis=0, tiled=...  7.28 us
  transfers between devices with their start and end apart: 8, of which 5 were waited for; matrix products, arithmetic and copies ran while one was open for 15% of the time, Pallas kernels for 0%

commit v1 on v0

--- a/solution.py
+++ b/solution.py
@@ -79,7 +79,12 @@
     )
     new_first, new_middle, new_last = (
         lax.all_to_all(updated[0], "member", split_axis=0, concat_axis=1, tiled=True),
-        lax.all_to_all(updated[1], "member", split_axis=0, concat_axis=1, tiled=True),
+        jnp.concatenate(
+            lax.all_to_all(
+                jnp.stack(jnp.split(updated[1], lax.axis_size("member"), axis=0)), "member", 0, 0
+            ),
+            axis=1,
+        ),
         lax.all_to_all(updated[2], "member", split_axis=0, concat_axis=1, tiled=True),
     )
     return (new_first, new_middle, new_last)

time: 350 us -> 367 us (1.049)
  local copies, waits for them, and re-layouts: 40.9 us -> 54.3 us
  waiting for transfers between devices: 181 us -> 194 us
  other arithmetic: 19.1 us -> 11.8 us
    split x0 -> x1, local copies, waits for them, and re-layouts: none -> 10.9 us  [on_device(): jnp.split(updated[1], lax.axis_size('member'), axis=0)]
    all_to_all x1, waiting for transfers between devices: 1.8 us -> 12 us  [on_device(): lax.all_to_all(updated[0], 'member', split_axis=0, concat_axis=1, tiled=T...]
    convert_element_type x3, other arithmetic: 10 us -> 3.2 us  [update_piece(): return renewed.astype(jnp.bfloat16).reshape(piece.shape)]
    reshape x0 -> x1, local copies, waits for them, and re-layouts: none -> 4.83 us  [on_device(): jnp.concatenate(lax.all_to_all(jnp.stack(jnp.split(updated[1], lax.axis_s...]
    all_to_all x1 -> x0, local copies, waits for them, and re-layouts: 4.83 us -> none  [on_device(): lax.all_to_all(updated[1], 'member', split_axis=0, concat_axis=1, tiled=T...]
    unnamed x36 -> x40, local copies, waits for them, and re-layouts: 23.7 us -> 27.2 us
  transfers between devices with their start and end apart: 8 -> 8, of which waited for: 5 -> 5; matrix products, arithmetic and copies ran while one was open for 15% -> 11% of each run, Pallas kernels for 0% -> 0%
where the time goes in v1:
time: 367 us
  waiting for transfers between devices  194 us (53%)
  local copies, waits for them, and re-layouts  54.3 us (15%)
  blocking collectives  43.1 us (12%)
  starting transfers between devices  29.8 us (8%)
  matrix products  19.3 us (5%)
  between operations  14.4 us (4%)
  other arithmetic  11.8 us (3%)
    all_to_all x1, waiting for transfers between devices, on_device(): lax.all_to_all(jnp.stack(jnp.split(updated[1], lax.axis_size('member'), a...  90.4 us
    all_to_all x1, waiting for transfers between devices, on_device(): lax.all_to_all(middle_weight, 'member', split_axis=1, concat_axis=0, tile...  80.1 us
    all_gather x1, blocking collectives, on_device(): every_member = lax.all_gather(scaled, 'member', axis=0, tiled=True)  30.8 us
    unnamed x40, local copies, waits for them, and re-layouts  27.2 us
    all_to_all x1, waiting for transfers between devices, on_device(): lax.all_to_all(updated[0], 'member', split_axis=0, concat_axis=1, tiled=T...  12 us
    dot_general x1, matrix products, on_device(): jnp.einsum('jsk,jkh->jsh', hidden_one, middle_full, preferred_element_typ...  10.9 us
    split x1, local copies, waits for them, and re-layouts, on_device(): jnp.split(updated[1], lax.axis_size('member'), axis=0)  10.9 us
  transfers between devices with their start and end apart: 8, of which 5 were waited for; matrix products, arithmetic and copies ran while one was open for 11% of the time, Pallas kernels for 0%

profile of v1, /device:TPU:0, one launch (start us, length us, event | category | flops | bytes accessed | tf_op | source)
XLA Modules:
  0.0 366.6 jit_solution(1965884118945550099)
XLA Ops:
  7.2 0.7 all-gather.4.cloned.1.call-update
  8.0 0.7 all-gather.6.cloned.1.call-update
  8.7 0.2 copy.49
  8.9 1.0 reshape.137
  9.9 7.3 %all-to-all-start.4 = ((bf16[8,2,640]{2,1,0:T(2,128)(2,1)}), bf16[8,2,640]{2,1,0:T(2,128)(2,1)S(1)}, u32[]{:S(2)}, u32[]{:S(2)}) async-start(bf16[8,2,640]{2,1,0:T(2,128)(2,1)} %reshape.137), calls=%async_computation.4 | async-start | bytes 40960 | tf_op jit(solution)/shard_map/all_to_all | solution.py:73
  17.2 1.3 copy.40
  18.5 5.3 %all-to-all-done.4 = bf16[8,2,640]{2,1,0:T(2,128)(2,1)S(1)} async-done(((bf16[8,2,640]{2,1,0:T(2,128)(2,1)}), bf16[8,2,640]{2,1,0:T(2,128)(2,1)S(1)}, u32[]{:S(2)}, u32[]{:S(2)}) %all-to-all-start.4) | async-done | bytes 20512 | tf_op jit(solution)/shard_map/all_to_all | solution.py:73
  23.8 3.5 all-to-all-start
  27.3 8.5 %copy.46 = bf16[2,512,2048]{2,0,1:T(2,128)(2,1)} copy(bf16[2,512,2048]{2,1,0:T(8,128)(2,1)} %param.12) | data formatting | bytes 8388608 | tf_op args[5]
  35.8 4.7 %all-to-all-done = bf16[2,256,512]{2,0,1:T(2,128)(2,1)S(1)} async-done(((bf16[2,256,512]{2,0,1:T(2,128)(2,1)}), bf16[2,256,512]{2,0,1:T(2,128)(2,1)S(1)}, u32[]{:S(2)}, u32[]{:S(2)}) %all-to-all-start) | async-done | bytes 524320 | tf_op jit(solution)/shard_map/all_to_all | solution.py:71
  40.5 4.6 %all-to-all-start.2 = ((bf16[2,512,2048]{2,0,1:T(2,128)(2,1)}), bf16[2,512,2048]{2,0,1:T(2,128)(2,1)}, u32[]{:S(2)}, u32[]{:S(2)}) async-start(bf16[2,512,2048]{2,0,1:T(2,128)(2,1)} %copy.46), calls=%async_computation.2 | async-start | bytes 8388608 | tf_op jit(solution)/shard_map/all_to_all | solution.py:72
  45.3 1.2 gather_fusion
  46.4 1.9 gather_fusion.1
  48.5 0.1 mul.94
  48.6 6.5 %all_gather.14 = bf16[2,2048,10]{1,2,0:T(8,128)(2,1)S(1)} all-gather(bf16[2,512,10]{1,2,0:T(8,128)(2,1)S(1)} %copy.42), channel_id=1, replica_groups=mesh['member'=8,'dp'=4] {'dp'}, dimensions={1}, use_global_device_ids=true | all-gather | bytes 102400 | tf_op jit(solution)/shard_map/all_gather | solution.py:41
  55.1 0.5 reshape.138
  55.7 0.3 reshape.111
  56.1 0.1 div.51
  56.3 0.3 copy.53
  56.7 80.1 %all-to-all-done.2 = bf16[2,512,2048]{2,0,1:T(2,128)(2,1)} async-done(((bf16[2,512,2048]{2,0,1:T(2,128)(2,1)}), bf16[2,512,2048]{2,0,1:T(2,128)(2,1)}, u32[]{:S(2)}, u32[]{:S(2)}) %all-to-all-start.2) | async-done | bytes 4194336 | tf_op jit(solution)/shard_map/all_to_all | solution.py:72
  136.8 4.1 %copy.47 = bf16[2,8,64,2048]{3,2,0,1:T(8,128)(2,1)S(1)} copy(bf16[2,8,64,2048]{3,0,2,1:T(2,128)(2,1)} %bitcast.12) | data formatting | bytes 8388608 | tf_op jit(solution)/shard_map/all_to_all | solution.py:72
  140.9 4.3 %copy.56 = bf16[2,8,64,2048]{3,1,2,0:T(8,128)(2,1)} copy(bf16[2,8,64,2048]{3,2,1,0:T(8,128)(2,1)S(1)} %bitcast.120) | data formatting | bytes 8388608
  145.2 4.2 %convert_reduce_fusion = f32[64,2048]{1,0:T(8,128)S(1)} fusion(bf16[2,8,64,2048]{3,0,2,1:T(2,128)(2,1)} %bitcast.12), kind=kLoop, calls=%fused_computation.6 | loop fusion | flops 4063232 | bytes 4718592 | tf_op jit(solution)/shard_map/reduce_sum | solution.py:20
  149.6 10.9 %tanh_convert_fusion = bf16[2,256,2048]{2,1,0:T(8,128)(2,1)} fusion(bf16[2,2048,2048]{2,1,0:T(8,128)(2,1)} %all-gather.6.cloned.1.call-done, bf16[2,256,2048]{2,1,0:T(8,128)(2,1)} %all-gather.4.cloned.1.call-done, bf16[256,256]{1,0:T(8,128)(2,1)S(1)} %gather_fusion), kind=kOutput, calls=%fused_computation.7 | convolution fusion | flops 4836032512 | bytes 21102592 | tf_op jit(solution)/shard_map/jsk,jkh->jsh/dot_general | solution.py:47
  160.5 2.2 convolution_multiply_fusion
  162.7 0.2 copy.43
  162.9 0.2 reshape.131
  163.1 30.8 %all-gather = f32[8,2,2560]{2,1,0:T(2,128)S(1)} all-gather(f32[1,2,2560]{2,1,0:T(2,128)S(1)} %reshape.131), channel_id=1, replica_groups=mesh['member'=8,'dp'=4] {'member'}, dimensions={0}, use_global_device_ids=true | all-gather | bytes 184320 | tf_op jit(solution)/shard_map/all_gather | solution.py:57
  193.9 0.1 reshape.132
  194.1 0.3 convolution_convert_fusion
  194.4 0.3 fusion.4
  194.7 5.8 %all-reduce = (bf16[16,16]{1,0:T(8,128)(2,1)S(1)}, bf16[16]{0:T(256)(128)(2,1)S(1)}) all-reduce(bf16[16,16]{1,0:T(8,128)(2,1)S(1)} %convolution_convert_fusion, bf16[16]{0:T(256)(128)(2,1)S(1)} %fusion.4), channel_id=1, replica_groups=mesh['member'=8,'dp'=4] {'dp'}, use_global_device_ids=true, to_apply=%region_1.0 | all-reduce | flops 272 | bytes 1088 | tf_op jit(solution)/shard_map/psum | solution.py:63
  200.6 1.5 cholesky.16
  202.1 0.6 compare_reduce_fusion
  202.7 0.6 fusion.18
  203.4 1.2 custom-call.10
  204.6 0.2 fusion.19
  204.8 0.2 fusion.20
  205.0 4.5 %fusion.29 = f32[32,131072]{1,0:T(8,128)S(1)} fusion(bf16[16,131072]{1,0:T(8,128)(2,1)} %bitcast.118, bf16[16,16]{0,1:T(8,128)(2,1)S(1)} %get-tuple-element.19, bf16[16,16]{0,1:T(8,128)(2,1)S(1)} %get-tuple-element.16), kind=kOutput, calls=%fused_computation.69 | convolution fusion | flops 134219776 | bytes 20972544 | tf_op jit(solution)/shard_map/dot_general | solution.py:17
  209.5 2.9 fusion.2
  212.4 10.9 %fusion.31 = (bf16[2,131072]{1,0:T(2,128)(2,1)S(1)}, bf16[2,131072]{1,0:T(2,128)(2,1)S(1)}, bf16[2,131072]{1,0:T(2,128)(2,1)S(1)}, bf16[2,131072]{1,0:T(2,128)(2...) fusion(bf16[16,131072]{1,0:T(8,128)(2,1)} %fusion.2), kind=kLoop, calls=%fused_computation.71 | loop fusion | bytes 8388608 | tf_op jit(solution)/shard_map/split | solution.py:84
  223.3 1.0 bitcast_dynamic-update-slice_fusion.7
  224.2 0.2 fusion.28
  224.5 0.5 reshape.112
  225.1 0.2 copy.51
  225.3 0.7 reshape.139
  226.0 3.7 %all-to-all-start.5 = ((bf16[8,2,640]{2,1,0:T(2,128)(2,1)}), bf16[8,2,640]{2,1,0:T(2,128)(2,1)S(1)}, u32[]{:S(2)}, u32[]{:S(2)}) async-start(bf16[8,2,640]{2,1,0:T(2,128)(2,1)} %reshape.139), calls=%async_computation.5 | async-start | bytes 40960 | tf_op jit(solution)/shard_map/all_to_all | solution.py:88
  229.7 0.5 fusion.30
  230.2 2.0 bitcast_dynamic-update-slice_fusion.6
  232.2 2.0 bitcast_dynamic-update-slice_fusion.5
  234.2 1.0 bitcast_dynamic-update-slice_fusion.4
  235.2 1.0 bitcast_dynamic-update-slice_fusion.3
  236.1 0.2 fusion.7
  236.4 1.0 bitcast_dynamic-update-slice_fusion.2
  237.3 0.9 copy.55
  238.3 6.0 %all-to-all-start.1 = ((bf16[16,32,512]{2,1,0:T(8,128)(2,1)}), bf16[16,32,512]{2,1,0:T(8,128)(2,1)S(1)}, u32[]{:S(2)}, u32[]{:S(2)}) async-start(bf16[16,32,512]{2,1,0:T(8,128)(2,1)} %bitcast.28), calls=%async_computation.1 | async-start | bytes 1048576 | tf_op jit(solution)/shard_map/all_to_all | solution.py:81
  244.3 1.0 bitcast_dynamic-update-slice_fusion.1
  245.2 1.0 bitcast_dynamic-update-slice_fusion
  246.2 12.0 %all-to-all-done.1 = bf16[16,32,512]{2,1,0:T(8,128)(2,1)S(1)} async-done(((bf16[16,32,512]{2,1,0:T(8,128)(2,1)}), bf16[16,32,512]{2,1,0:T(8,128)(2,1)S(1)}, u32[]{:S(2)}, u32[]{:S(2)}) %all-to-all-start.1) | async-done | bytes 524320 | tf_op jit(solution)/shard_map/all_to_all | solution.py:81
  258.2 4.6 %all-to-all-start.3 = ((bf16[8,2,64,2048]{3,2,1,0:T(8,128)(2,1)}), bf16[8,2,64,2048]{3,2,1,0:T(8,128)(2,1)}, u32[]{:S(2)}, u32[]{:S(2)}) async-start(bf16[8,2,64,2048]{3,2,1,0:T(8,128)(2,1)} %bitcast_dynamic-update-slice_fusion), calls=%async_computation.3 | async-start | bytes 8388608 | tf_op jit(solution)/shard_map/all_to_all | solution.py:83
  262.9 0.7 all_to_all.79
  263.6 0.8 copy.45
  264.5 90.4 %all-to-all-done.3 = bf16[8,2,64,2048]{3,2,1,0:T(8,128)(2,1)} async-done(((bf16[8,2,64,2048]{3,2,1,0:T(8,128)(2,1)}), bf16[8,2,64,2048]{3,2,1,0:T(8,128)(2,1)}, u32[]{:S(2)}, u32[]{:S(2)}) %all-to-all-start.3) | async-done | bytes 4194336 | tf_op jit(solution)/shard_map/all_to_all | solution.py:83
  354.9 4.8 %copy.48 = bf16[2,8,64,2048]{3,2,1,0:T(8,128)(2,1)} copy(bf16[2,8,64,2048]{3,2,0,1:T(8,128)(2,1)} %bitcast.14) | data formatting | bytes 8388608 | tf_op jit(solution)/shard_map/reshape | solution.py:82
  (49 shorter events, 1.1 us)
Async XLA Ops:
  7.2 38.1 %copy-start = (bf16[512,256]{1,0:T(8,128)(2,1)S(1)}, bf16[512,256]{1,0:T(8,128)(2,1)}, u32[]{:S(2)}) copy-start(bf16[512,256]{1,0:T(8,128)(2,1)} %param.7) | copy-start | bytes 786436
  7.2 10.0 %copy-start.5 = (bf16[2,256,512]{2,1,0:T(8,128)(2,1)S(1)}, bf16[2,256,512]{2,1,0:T(8,128)(2,1)}, u32[]{:S(2)}) copy-start(bf16[2,256,512]{2,1,0:T(8,128)(2,1)} %param.11) | copy-start | bytes 1572868
  7.2 1.5 copy-start.6
  7.2 142.4 %all-gather.4.cloned.1.call-start = ((), (), s32[]{:S(2)}) async-start(), calls=%async_computation.6 | async-start | bytes 2621440 | tf_op jit(solution)/shard_map/all_gather | solution.py:39
  7.9 141.6 %all-gather.6.cloned.1.call-start = ((), (), s32[]{:S(2)}) async-start(), calls=%async_computation.7 | async-start | bytes 20971520 | tf_op jit(solution)/shard_map/all_gather | solution.py:40
  9.9 13.9 %all-to-all-start.4 = ((bf16[8,2,640]{2,1,0:T(2,128)(2,1)}), bf16[8,2,640]{2,1,0:T(2,128)(2,1)S(1)}, u32[]{:S(2)}, u32[]{:S(2)}) async-start(bf16[8,2,640]{2,1,0:T(2,128)(2,1)} %reshape.137), calls=%async_computation.4 | async-start | bytes 40960 | tf_op jit(solution)/shard_map/all_to_all | solution.py:73
  23.8 16.8 %all-to-all-start = ((bf16[2,256,512]{2,0,1:T(2,128)(2,1)}), bf16[2,256,512]{2,0,1:T(2,128)(2,1)S(1)}, u32[]{:S(2)}, u32[]{:S(2)}) async-start(bf16[2,256,512]{2,0,1:T(2,128)(2,1)} %copy.40), calls=%async_computation | async-start | bytes 1048576 | tf_op jit(solution)/shard_map/all_to_all | solution.py:71
  35.8 9.4 %copy-start.7 = (s32[256]{0:T(256)S(1)}, s32[256]{0:T(256)}, u32[]{:S(2)}) copy-start(s32[256]{0:T(256)} %param.9) | copy-start | bytes 3076
  35.8 10.6 %copy-start.2 = (s32[512]{0:T(512)S(1)}, s32[512]{0:T(512)}, u32[]{:S(2)}) copy-start(s32[512]{0:T(512)} %param.8) | copy-start | bytes 6148
  35.8 12.5 %copy-start.8 = (f32[10]{0:T(128)S(1)}, f32[10]{0:T(128)}, u32[]{:S(2)}) copy-start(f32[10]{0:T(128)} %param.10) | copy-start | bytes 124
  40.5 96.3 %all-to-all-start.2 = ((bf16[2,512,2048]{2,0,1:T(2,128)(2,1)}), bf16[2,512,2048]{2,0,1:T(2,128)(2,1)}, u32[]{:S(2)}, u32[]{:S(2)}) async-start(bf16[2,512,2048]{2,0,1:T(2,128)(2,1)} %copy.46), calls=%async_computation.2 | async-start | bytes 8388608 | tf_op jit(solution)/shard_map/all_to_all | solution.py:72
  205.0 4.5 %copy-start.3 = (bf16[2,8,64,2048]{3,1,2,0:T(8,128)(2,1)S(1)}, bf16[2,8,64,2048]{3,1,2,0:T(8,128)(2,1)}, u32[]{:S(2)}) copy-start(bf16[2,8,64,2048]{3,1,2,0:T(8,128)(2,1)} %copy.56) | copy-start | bytes 12582916
  226.0 12.3 %all-to-all-start.5 = ((bf16[8,2,640]{2,1,0:T(2,128)(2,1)}), bf16[8,2,640]{2,1,0:T(2,128)(2,1)S(1)}, u32[]{:S(2)}, u32[]{:S(2)}) async-start(bf16[8,2,640]{2,1,0:T(2,128)(2,1)} %reshape.139), calls=%async_computation.5 | async-start | bytes 40960 | tf_op jit(solution)/shard_map/all_to_all | solution.py:88
  229.7 4.5 %copy-start.4 = (bf16[2,131072]{1,0:T(2,128)(2,1)S(1)}, bf16[2,131072]{1,0:T(2,128)(2,1)}, u32[]{:S(2)}) copy-start(bf16[2,131072]{1,0:T(2,128)(2,1)} %get-tuple-element.9) | copy-start | bytes 1572868
  238.3 19.9 %all-to-all-start.1 = ((bf16[16,32,512]{2,1,0:T(8,128)(2,1)}), bf16[16,32,512]{2,1,0:T(8,128)(2,1)S(1)}, u32[]{:S(2)}, u32[]{:S(2)}) async-start(bf16[16,32,512]{2,1,0:T(8,128)(2,1)} %bitcast.28), calls=%async_computation.1 | async-start | bytes 1048576 | tf_op jit(solution)/shard_map/all_to_all | solution.py:81
  258.2 96.7 %all-to-all-start.3 = ((bf16[8,2,64,2048]{3,2,1,0:T(8,128)(2,1)}), bf16[8,2,64,2048]{3,2,1,0:T(8,128)(2,1)}, u32[]{:S(2)}, u32[]{:S(2)}) async-start(bf16[8,2,64,2048]{3,2,1,0:T(8,128)(2,1)} %bitcast_dynamic-update-slice_fusion), calls=%async_computation.3 | async-start | bytes 8388608 | tf_op jit(solution)/shard_map/all_to_all | solution.py:83
  354.9 4.8 %copy-start.1 = (bf16[512,256]{1,0:T(8,128)(2,1)S(1)}, bf16[512,256]{1,0:T(8,128)(2,1)}, u32[]{:S(2)}) copy-start(bf16[512,256]{1,0:T(8,128)(2,1)} %param.7) | copy-start | bytes 786436
Sparse Core Ops, SparseCore 0:
  9.6 25.2 all-gather.3
  36.5 106.5 all-gather.5
